TPU v7x, 256 devices: a whole 4x4x8 slice. The times are simulated.
256 devices in a mesh: seq: 64 (over z_hi, y, x), ch: 4 (over z_lo, core).
Axes of the slice: x: 4, y: 4, z: 8 (z_hi: 4, z_lo: 2; z = z_hi * 2 + z_lo), core: 2. Of those that a mesh axis runs over, the one named last changes fastest.
Arguments:
- inputs: float32 [256, 32768], P('ch', 'seq'), may hold values from -6 to 6
- w_in: float32 [3, 256, 256], P(None, 'ch'), may hold values from -0.375 to 0.375
- short_w: float32 [3, 3, 256], P(None, None, 'ch'), may hold values from -3 to 3
- filter_param: float32 [256, 32768], P('ch', 'seq'), may hold values from -6 to 6
- skip: float32 [256], P('ch'), may hold values from -4 to 4
- w_out: float32 [256, 256], P('ch'), may hold values from -0.375 to 0.375
- cotangent: float32 [256, 32768], P('ch', 'seq'), may hold values from -6 to 6
Outputs:
- output: float32 [256, 32768], P('ch', 'seq')
- grad_input: float32 [256, 32768], P('ch', 'seq')
- grad_filter: float32 [256, 32768], P('ch', 'seq')
All inputs are finite; a program needn't handle non-finite values.
Results may differ from a plain program's by a relative error of at most 0.0003.
Values sent between devices are 32-bit elements; how exact they have to be, the bound alone decides.
No kernel may reach another device: no remote copies, remote signals or barrier semaphores. Data moves between devices by JAX's collectives and lax.ppermute only.
A program may use at most 64 MiB of HBM per device.

v0:
```python
import math
import jax
import jax.numpy as jnp
from jax import lax
from jax.sharding import PartitionSpec as P

PRECISE = lax.Precision.HIGHEST


def passed_along(block, axis, distance):
    devices = range(lax.axis_size(axis))
    route = [(i - distance, i) for i in devices if i - distance in devices]
    return lax.ppermute(block, axis, route)


def fourier_tables(order):
    indices = jnp.arange(order, dtype=jnp.int32)
    products = indices[:, None] * indices[None, :] % order
    angles = products.astype(jnp.float32) * (2.0 * math.pi / order)
    return (jnp.cos(angles), jnp.sin(angles))


def to_sorted(spec_real, spec_imag):
    count, channels, length = spec_real.shape
    shards = lax.axis_size("seq")
    stacked = jnp.concatenate([spec_real, spec_imag], 0).reshape(
        2 * count, channels, shards, length // shards
    )
    arrived = lax.all_to_all(stacked, "seq", split_axis=2, concat_axis=2, tiled=True)
    arrived = jnp.transpose(arrived, (0, 1, 3, 2)).reshape(2 * count, channels, length)
    return (arrived[:count], arrived[count:])


def from_sorted(spec_real, spec_imag):
    count, channels, length = spec_real.shape
    shards = lax.axis_size("seq")
    stacked = jnp.concatenate([spec_real, spec_imag], 0).reshape(
        2 * count, channels, length // shards, shards
    )
    stacked = jnp.transpose(stacked, (0, 1, 3, 2))
    arrived = lax.all_to_all(stacked, "seq", split_axis=2, concat_axis=2, tiled=True).reshape(
        2 * count, channels, length
    )
    return (arrived[:count], arrived[count:])


def to_spectrum(signal, tables):
    cos_small, sin_small, cos_big, sin_big = tables
    rows_in, channels, length = signal.shape
    shards = lax.axis_size("seq")
    slab_len = length // shards
    full_len = length * shards
    blocks = lax.all_to_all(
        signal.reshape(rows_in, channels, shards, slab_len),
        "seq",
        split_axis=2,
        concat_axis=2,
        tiled=True,
    )
    part_real = jnp.einsum("ks,ncsm->nckm", cos_small, blocks, precision=PRECISE)
    part_imag = -jnp.einsum("ks,ncsm->nckm", sin_small, blocks, precision=PRECISE)
    count = part_real.shape[0]
    positions = lax.axis_index("seq") * slab_len + jnp.arange(slab_len, dtype=jnp.int32)
    residues = jnp.arange(shards, dtype=jnp.int32)
    angles = (residues[:, None] * positions[None, :] % full_len).astype(jnp.float32) * (
        2.0 * math.pi / full_len
    )
    turn_cos = jnp.cos(angles)
    turn_sin = jnp.sin(angles)
    rot_real = part_real * turn_cos + part_imag * turn_sin
    rot_imag = part_imag * turn_cos - part_real * turn_sin
    stacked = jnp.concatenate([rot_real, rot_imag], 0)
    arrived = lax.all_to_all(stacked, "seq", split_axis=2, concat_axis=2, tiled=True).reshape(
        2 * count, channels, length
    )
    row_real = arrived[:count]
    row_imag = arrived[count:]
    spec_real = jnp.einsum("ncj,jk->nck", row_real, cos_big, precision=PRECISE) + jnp.einsum(
        "ncj,jk->nck", row_imag, sin_big, precision=PRECISE
    )
    spec_imag = jnp.einsum("ncj,jk->nck", row_imag, cos_big, precision=PRECISE) - jnp.einsum(
        "ncj,jk->nck", row_real, sin_big, precision=PRECISE
    )
    spec_real, spec_imag = to_sorted(spec_real, spec_imag)
    return (spec_real, spec_imag)


def from_spectrum(spec_real, spec_imag, tables):
    cos_small, sin_small, cos_big, sin_big = tables
    spec_real, spec_imag = from_sorted(spec_real, spec_imag)
    count, channels, length = spec_real.shape
    shards = lax.axis_size("seq")
    slab_len = length // shards
    full_len = length * shards
    row_real = jnp.einsum("nck,kj->ncj", spec_real, cos_big, precision=PRECISE) - jnp.einsum(
        "nck,kj->ncj", spec_imag, sin_big, precision=PRECISE
    )
    row_imag = jnp.einsum("nck,kj->ncj", spec_imag, cos_big, precision=PRECISE) + jnp.einsum(
        "nck,kj->ncj", spec_real, sin_big, precision=PRECISE
    )
    positions = jnp.arange(length, dtype=jnp.int32)
    angles = (positions * lax.axis_index("seq") % full_len).astype(jnp.float32) * (
        2.0 * math.pi / full_len
    )
    turn_cos = jnp.cos(angles)
    turn_sin = jnp.sin(angles)
    rot_real = row_real * turn_cos - row_imag * turn_sin
    rot_imag = row_imag * turn_cos + row_real * turn_sin
    stacked = jnp.concatenate([rot_real, rot_imag], 0).reshape(
        2 * count, channels, shards, slab_len
    )
    arrived = lax.all_to_all(stacked, "seq", split_axis=2, concat_axis=2, tiled=True)
    arrived_real = arrived[:count]
    arrived_imag = arrived[count:]
    pieces = (
        jnp.einsum("sk,nckm->ncsm", cos_small, arrived_real, precision=PRECISE)
        - jnp.einsum("sk,nckm->ncsm", sin_small, arrived_imag, precision=PRECISE)
    ) / full_len
    restored = lax.all_to_all(pieces, "seq", split_axis=2, concat_axis=2, tiled=True)
    return restored.reshape(pieces.shape[0], channels, length)


def body(inputs, w_in, short_w, filter_param, skip, w_out, cotangent):
    channels, length = inputs.shape
    shards = lax.axis_size("seq")
    filter_scale = (length * shards) ** (-0.5)
    cos_small, sin_small = fourier_tables(shards)
    cos_big, sin_big = fourier_tables(length)
    tables = (cos_small, sin_small, cos_big, sin_big)
    columns = w_in
    projected = jnp.einsum(
        "icd,dt->ict", columns, lax.all_gather(inputs, "ch", axis=0, tiled=True), precision=PRECISE
    )
    tap_first = short_w[0][:, :, None]
    tap_second = short_w[1][:, :, None]
    tap_third = short_w[2][:, :, None]
    before = passed_along(projected[:, :, length - 2 :], "seq", 1)
    widened = jnp.concatenate([before, projected], 2)
    convolved = (
        tap_first * projected
        + tap_second * widened[:, :, 1 : length + 1]
        + tap_third * widened[:, :, 0:length]
    )
    gated = convolved[1] * convolved[2]
    filter_taps = filter_param * filter_scale
    spec_real, spec_imag = to_spectrum(jnp.stack([gated, filter_taps]), tables)
    gated_real, gated_imag = (spec_real[0], spec_imag[0])
    filt_real, filt_imag = (spec_real[1], spec_imag[1])
    prod_real = filt_real * gated_real - filt_imag * gated_imag
    prod_imag = filt_real * gated_imag + filt_imag * gated_real
    convolution = from_spectrum(prod_real[None], prod_imag[None], tables)[0]
    mixed = convolution + skip[:, None] * gated
    out_gate = convolved[0] * mixed
    columns = w_out
    output = jnp.dot(columns, lax.all_gather(out_gate, "ch", axis=0, tiled=True), precision=PRECISE)
    columns = w_out
    grad_gate = lax.psum_scatter(
        jnp.dot(columns.T, cotangent, precision=PRECISE), "ch", scatter_dimension=0, tiled=True
    )
    grad_mixed = convolved[0] * grad_gate
    grad_first = mixed * grad_gate
    grad_spec_real, grad_spec_imag = to_spectrum(grad_mixed[None], tables)
    grad_real = grad_spec_real[0]
    grad_imag = grad_spec_imag[0]
    corr_real = filt_real * grad_real + filt_imag * grad_imag
    corr_imag = filt_real * grad_imag - filt_imag * grad_real
    taps_real = grad_real * gated_real + grad_imag * gated_imag
    taps_imag = grad_imag * gated_real - grad_real * gated_imag
    restored = from_spectrum(
        jnp.stack([corr_real, taps_real]), jnp.stack([corr_imag, taps_imag]), tables
    )
    grad_gated = restored[0] + skip[:, None] * grad_mixed
    grad_filter = restored[1] * filter_scale
    grad_conv = jnp.stack([grad_first, grad_gated * convolved[2], grad_gated * convolved[1]])
    beyond = passed_along(grad_conv[:, :, 0:2], "seq", -1)
    extended = jnp.concatenate([grad_conv, beyond], 2)
    grad_proj = (
        tap_first * grad_conv
        + tap_second * extended[:, :, 1 : length + 1]
        + tap_third * extended[:, :, 2 : length + 2]
    )
    columns = w_in
    grad_input = lax.psum_scatter(
        jnp.einsum("icd,ict->dt", columns, grad_proj, precision=PRECISE),
        "ch",
        scatter_dimension=0,
        tiled=True,
    )
    return (output, grad_input, grad_filter)


def solution(mesh):
    in_specs = (
        P("ch", "seq"),
        P(None, "ch", None),
        P(None, None, "ch"),
        P("ch", "seq"),
        P("ch"),
        P("ch", None),
        P("ch", "seq"),
    )
    out_specs = (P("ch", "seq"), P("ch", "seq"), P("ch", "seq"))
    return jax.shard_map(body, mesh=mesh, in_specs=in_specs, out_specs=out_specs, check_vma=False)
```

profile of v0, /device:TPU:1, one launch (start us, length us, event | category | flops | bytes accessed | tf_op | source)
XLA Modules:
  0.0 433.5 jit_solution(6016858753336470031)
XLA Ops:
  7.2 9.9 %all_gather.6 = f32[256,512]{1,0:T(8,128)S(1)} all-gather(f32[64,512]{1,0:T(8,128)} %param.7), channel_id=1, replica_groups=mesh['seq'=64,'ch'=4] {'ch'}, dimensions={0}, use_global_device_ids=true | all-gather | bytes 655360 | tf_op jit(solution)/shard_map/all_gather | solution.py:132
  23.8 17.3 %all-to-all-start = ((f32[64,1,1024]{2,1,0:T(1,128)}), f32[64,1,1024]{2,1,0:T(1,128)S(1)}, u32[]{:S(2)}, u32[]{:S(2)}) async-start(f32[64,1,1024]{2,1,0:T(1,128)} %reshape.218), calls=%async_computation | async-start | bytes 524288 | tf_op jit(solution)/shard_map/all_to_all | solution.py:53
  41.3 13.2 %all-to-all-done = f32[64,1,1024]{2,1,0:T(1,128)S(1)} async-done(((f32[64,1,1024]{2,1,0:T(1,128)}), f32[64,1,1024]{2,1,0:T(1,128)S(1)}, u32[]{:S(2)}, u32[]{:S(2)}) %all-to-all-start) | async-done | bytes 262176 | tf_op jit(solution)/shard_map/all_to_all | solution.py:53
  59.8 24.5 %all_to_all.60 = f32[64,1,2048]{2,1,0:T(1,128)S(1)} all-to-all(f32[64,1,2048]{2,1,0:T(1,128)S(1)} %reshape.220), channel_id=1, replica_groups=mesh['seq'=64,'ch'=4] {'seq'}, dimensions={0} | all-to-all | bytes 1048576 | tf_op jit(solution)/shard_map/all_to_all | solution.py:73
  86.7 5.4 %fusion.19 = f32[2,64,512]{2,1,0:T(8,128)S(1)} fusion(f32[2,64,64,8]{1,3,0,2:T(8,128)S(1)} %get-tuple-element.26), kind=kOutput, calls=%fused_computation.40 | convolution fusion | flops 406323200 | bytes 524288 | tf_op jit(solution)/shard_map/ncj,jk->nck/dot_general | solution.py:78
  92.1 5.4 %fusion.17 = f32[2,64,512]{2,1,0:T(8,128)S(1)} fusion(f32[2,64,64,8]{1,3,0,2:T(8,128)S(1)} %get-tuple-element.27), kind=kOutput, calls=%fused_computation.38 | convolution fusion | flops 406323200 | bytes 524288 | tf_op jit(solution)/shard_map/ncj,jk->nck/dot_general | solution.py:81
  97.6 5.5 %convolution_add_fusion.1 = f32[2,64,512]{2,1,0:T(8,128)S(1)} fusion(f32[2,64,512]{2,1,0:T(8,128)S(1)} %fusion.19, f32[2,64,64,8]{1,3,0,2:T(8,128)S(1)} %get-tuple-element.27), kind=kOutput, calls=%fused_computation.16 | convolution fusion | flops 406388736 | bytes 786432 | tf_op jit(solution)/shard_map/ncj,jk->nck/dot_general | solution.py:78
  103.1 5.7 %convolution_subtract_fusion.3 = f32[2,64,512]{2,1,0:T(8,128)S(1)} fusion(f32[2,64,512]{2,1,0:T(8,128)S(1)} %fusion.17, f32[2,64,64,8]{1,3,0,2:T(8,128)S(1)} %get-tuple-element.26), kind=kOutput, calls=%fused_computation.15 | convolution fusion | flops 406388736 | bytes 786432 | tf_op jit(solution)/shard_map/ncj,jk->nck/dot_general | solution.py:81
  109.9 21.4 %all_to_all.61 = f32[64,1,2048]{2,1,0:T(1,128)S(1)} all-to-all(f32[64,1,2048]{2,1,0:T(1,128)S(1)} %reshape.222), channel_id=1, replica_groups=mesh['seq'=64,'ch'=4] {'seq'}, dimensions={0} | all-to-all | bytes 1048576 | tf_op jit(solution)/shard_map/all_to_all | solution.py:29
  134.9 7.1 %all-to-all-start.3 = ((f32[64,1,1024]{2,1,0:T(1,128)}), f32[64,1,1024]{2,1,0:T(1,128)S(1)}, u32[]{:S(2)}, u32[]{:S(2)}) async-start(f32[64,1,1024]{2,1,0:T(1,128)} %reshape.224), calls=%async_computation.3 | async-start | bytes 524288 | tf_op jit(solution)/shard_map/all_to_all | solution.py:41
  142.0 12.3 %all-to-all-done.3 = f32[64,1,1024]{2,1,0:T(1,128)S(1)} async-done(((f32[64,1,1024]{2,1,0:T(1,128)}), f32[64,1,1024]{2,1,0:T(1,128)S(1)}, u32[]{:S(2)}, u32[]{:S(2)}) %all-to-all-start.3) | async-done | bytes 262176 | tf_op jit(solution)/shard_map/all_to_all | solution.py:41
  182.9 10.5 %all-to-all-done.4 = f32[64,1,1024]{2,1,0:T(1,128)S(1)} async-done(((f32[64,1,1024]{2,1,0:T(1,128)}), f32[64,1,1024]{2,1,0:T(1,128)S(1)}, u32[]{:S(2)}, u32[]{:S(2)}) %all-to-all-start.4) | async-done | bytes 262176 | tf_op jit(solution)/shard_map/all_to_all | solution.py:112
  196.5 15.9 %all_to_all.62 = f32[64,1,512]{2,1,0:T(1,128)S(1)} all-to-all(f32[64,1,512]{2,1,0:T(1,128)S(1)} %reshape.228), channel_id=1, replica_groups=mesh['seq'=64,'ch'=4] {'seq'}, dimensions={0} | all-to-all | bytes 262144 | tf_op jit(solution)/shard_map/all_to_all | solution.py:119
  216.2 19.7 %all_to_all.63 = f32[64,1,512]{2,1,0:T(1,128)S(1)} all-to-all(f32[64,1,512]{2,1,0:T(1,128)S(1)} %reshape.230), channel_id=1, replica_groups=mesh['seq'=64,'ch'=4] {'seq'}, dimensions={0} | all-to-all | bytes 262144 | tf_op jit(solution)/shard_map/all_to_all | solution.py:53
  238.8 17.0 %all_to_all.64 = f32[64,1,1024]{2,1,0:T(1,128)S(1)} all-to-all(f32[64,1,1024]{2,1,0:T(1,128)S(1)} %reshape.232), channel_id=1, replica_groups=mesh['seq'=64,'ch'=4] {'seq'}, dimensions={0} | all-to-all | bytes 524288 | tf_op jit(solution)/shard_map/all_to_all | solution.py:73
  277.1 16.9 %all_to_all.65 = f32[64,1,1024]{2,1,0:T(1,128)S(1)} all-to-all(f32[64,1,1024]{2,1,0:T(1,128)S(1)} %reshape.234), channel_id=1, replica_groups=mesh['seq'=64,'ch'=4] {'seq'}, dimensions={0} | all-to-all | bytes 524288 | tf_op jit(solution)/shard_map/all_to_all | solution.py:29
  296.4 19.1 %all_to_all.66 = f32[64,1,2048]{2,1,0:T(1,128)S(1)} all-to-all(f32[64,1,2048]{2,1,0:T(1,128)S(1)} %reshape.236), channel_id=1, replica_groups=mesh['seq'=64,'ch'=4] {'seq'}, dimensions={0} | all-to-all | bytes 1048576 | tf_op jit(solution)/shard_map/all_to_all | solution.py:41
  323.3 5.4 %fusion.15 = f32[2,64,512]{2,1,0:T(8,128)S(1)} fusion(f32[2,64,64,8]{1,3,0,2:T(8,128)S(1)} %get-tuple-element.23), kind=kOutput, calls=%fused_computation.36 | convolution fusion | flops 406323200 | bytes 524288 | tf_op jit(solution)/shard_map/nck,kj->ncj/dot_general | solution.py:95
  328.8 5.5 %convolution_subtract_fusion.1 = f32[2,64,512]{2,1,0:T(8,128)S(1)} fusion(f32[2,64,512]{2,1,0:T(8,128)S(1)} %fusion.15, f32[2,64,64,8]{1,3,0,2:T(8,128)S(1)} %get-tuple-element.22), kind=kOutput, calls=%fused_computation.11 | convolution fusion | flops 406388736 | bytes 786432 | tf_op jit(solution)/shard_map/nck,kj->ncj/dot_general | solution.py:95
  334.3 5.7 %multiply_subtract_fusion.1 = (f32[2,64,512]{2,1,0:T(8,128)S(1)}, f32[2,64,512]{2,1,0:T(8,128)S(1)}) fusion(f32[2,64,512]{2,1,0:T(8,128)S(1)} %convolution_subtract_fusion.1, f32[512]{0:T(512)S(1)} %get-tuple-element.47, f32[512]{0:T(512)S(1)} %get-tuple-element.48, f32[2,64,512]{2,1,0:T(8,128)S(1)} %fusion.13, f32[2,64,64,8]{1,3,0,2:T(8,128)S(1)} %get-tuple-element.23), kind=kOutput, calls=%fused_computation.109 | convolution fusion | flops 406781952 | bytes 1314816 | tf_op jit(solution)/shard_map/nck,kj->ncj/dot_general | solution.py:98
  341.1 19.7 %all_to_all.67 = f32[64,1,2048]{2,1,0:T(1,128)S(1)} all-to-all(f32[64,1,2048]{2,1,0:T(1,128)S(1)} %reshape.238), channel_id=1, replica_groups=mesh['seq'=64,'ch'=4] {'seq'}, dimensions={0} | all-to-all | bytes 1048576 | tf_op jit(solution)/shard_map/all_to_all | solution.py:112
  366.2 17.7 %all_to_all.68 = f32[64,1,1024]{2,1,0:T(1,128)S(1)} all-to-all(f32[64,1,1024]{2,1,0:T(1,128)S(1)} %reshape.240), channel_id=1, replica_groups=mesh['seq'=64,'ch'=4] {'seq'}, dimensions={0} | all-to-all | bytes 524288 | tf_op jit(solution)/shard_map/all_to_all | solution.py:119
  395.2 17.1 %all_gather.7 = f32[256,512]{1,0:T(8,128)S(1)} all-gather(f32[64,512]{1,0:T(8,128)S(1)} %get-tuple-element.39), channel_id=1, replica_groups=mesh['seq'=64,'ch'=4] {'ch'}, dimensions={0}, use_global_device_ids=true | all-gather | bytes 655360 | tf_op jit(solution)/shard_map/all_gather | solution.py:155
  413.4 13.1 %reduce-scatter.7.cloned.1.call-done = f32[64,512]{1,0:T(8,128)} async-done(((f32[256,512]{1,0:T(8,128)}), f32[64,512]{1,0:T(8,128)}) %reduce-scatter.7.cloned.1.call-update) | async-done | bytes 131088
  (138 shorter events, 107.3 us)
Async XLA Ops:
  7.2 9.9 %copy-start = (f32[3,64,256]{2,1,0:T(8,128)S(1)}, f32[3,64,256]{2,1,0:T(8,128)}, u32[]{:S(2)}) copy-start(f32[3,64,256]{2,1,0:T(8,128)} %param.8) | copy-start | bytes 589828
  17.6 2.6 copy-start.3
  17.7 4.5 %collective-permute-start = (f32[3,64,2]{2,1,0:T(8,128)S(1)}, f32[3,64,2]{2,1,0:T(8,128)S(1)}, u32[]{:S(2)}, u32[]{:S(2)}) collective-permute-start(f32[3,64,2]{2,1,0:T(8,128)S(1)} %slice.167), channel_id=1, source_target_pairs={{0,4},{4,8},{8,12},{12,16},{16,20},{20,24},{24,28},{28,32},{32,36}... | collective-permute-start | bytes 4616 | tf_op jit(solution)/shard_map/ppermute | solution.py:13
  20.3 0.7 copy-start.5
  23.8 30.6 %all-to-all-start = ((f32[64,1,1024]{2,1,0:T(1,128)}), f32[64,1,1024]{2,1,0:T(1,128)S(1)}, u32[]{:S(2)}, u32[]{:S(2)}) async-start(f32[64,1,1024]{2,1,0:T(1,128)} %reshape.218), calls=%async_computation | async-start | bytes 524288 | tf_op jit(solution)/shard_map/all_to_all | solution.py:53
  134.9 19.4 %all-to-all-start.3 = ((f32[64,1,1024]{2,1,0:T(1,128)}), f32[64,1,1024]{2,1,0:T(1,128)S(1)}, u32[]{:S(2)}, u32[]{:S(2)}) async-start(f32[64,1,1024]{2,1,0:T(1,128)} %reshape.224), calls=%async_computation.3 | async-start | bytes 524288 | tf_op jit(solution)/shard_map/all_to_all | solution.py:41
  176.4 5.0 %copy-start.2 = (f32[64,256]{1,0:T(8,128)S(1)}, f32[64,256]{1,0:T(8,128)}, u32[]{:S(2)}) copy-start(f32[64,256]{1,0:T(8,128)} %param.12) | copy-start | bytes 196612
  176.4 5.0 %copy-start.4 = (f32[64,512]{1,0:T(8,128)S(1)}, f32[64,512]{1,0:T(8,128)}, u32[]{:S(2)}) copy-start(f32[64,512]{1,0:T(8,128)} %param.13) | copy-start | bytes 393220
  176.4 17.0 %all-to-all-start.4 = ((f32[64,1,1024]{2,1,0:T(1,128)}), f32[64,1,1024]{2,1,0:T(1,128)S(1)}, u32[]{:S(2)}, u32[]{:S(2)}) async-start(f32[64,1,1024]{2,1,0:T(1,128)} %reshape.226), calls=%async_computation.4 | async-start | bytes 524288 | tf_op jit(solution)/shard_map/all_to_all | solution.py:112
  181.2 32.5 %reduce-scatter.5.cloned.1.call-start = ((), (), s32[]{:S(2)}) async-start(), calls=%async_computation.14 | async-start | bytes 655360 | tf_op jit(solution)/shard_map/reduce_scatter | solution.py:157
  182.8 243.7 %reduce-scatter.7.cloned.1.call-start = ((), (), s32[]{:S(2)}) async-start(), calls=%async_computation.15 | async-start | bytes 655360
  213.5 0.7 copy-start.6
  385.3 0.9 copy-start.1
  386.4 5.7 %collective-permute-start.1 = (f32[3,64,2]{2,1,0:T(8,128)S(1)}, f32[3,64,2]{2,1,0:T(8,128)S(1)}, u32[]{:S(2)}, u32[]{:S(2)}) collective-permute-start(f32[3,64,2]{2,1,0:T(8,128)S(1)} %slice.192), channel_id=1, source_target_pairs={{4,0},{8,4},{12,8},{16,12},{20,16},{24,20},{28,24},{32,28},{36,32}... | collective-permute-start | bytes 4616 | tf_op jit(solution)/shard_map/ppermute | solution.py:13
Sparse Core Ops, SparseCore 0:
  184.5 26.0 reduce-scatter.4
  394.5 31.9 reduce-scatter.6
where the time goes:
time: 440 us; the launch traced here: 434 us
  blocking collectives  199 us (45%)
  matrix products  92.8 us (21%)
  waiting for transfers between devices  54.6 us (12%)
  starting transfers between devices  33.2 us (8%)
  other arithmetic  20.1 us (5%)
  local copies, waits for them, and re-layouts  18.8 us (4%)
  between operations  15.1 us (3%)
    all_to_all x2, blocking collectives, to_spectrum(): lax.all_to_all(stacked, 'seq', split_axis=2, concat_axis=2, tiled=True)  41.5 us
    all_to_all x2, blocking collectives, to_sorted(): lax.all_to_all(stacked, 'seq', split_axis=2, concat_axis=2, tiled=True)  38.4 us
    all_to_all x2, blocking collectives, from_spectrum(): lax.all_to_all(pieces, 'seq', split_axis=2, concat_axis=2, tiled=True)  33.6 us
    all_to_all x1, blocking collectives, from_spectrum(): lax.all_to_all(stacked, 'seq', split_axis=2, concat_axis=2, tiled=True)  19.7 us
    all_to_all x1, blocking collectives, to_spectrum(): lax.all_to_all(signal.reshape(rows_in, channels, shards, slab_len), 'seq'...  19.7 us
    all_to_all x1, blocking collectives, from_sorted(): lax.all_to_all(stacked, 'seq', split_axis=2, concat_axis=2, tiled=True)  19.1 us
    all_to_all x1, starting transfers between devices, to_spectrum(): lax.all_to_all(signal.reshape(rows_in, channels, shards, slab_len), 'seq'...  17.3 us
    all_gather x1, blocking collectives, body(): lax.all_gather(out_gate, 'ch', axis=0, tiled=True)  17.1 us
  transfers between devices with their start and end apart: 7, of which 6 were waited for; matrix products, arithmetic and copies ran while one was open for 2% of the time, Pallas kernels for 0%

commit v1 on v0

--- a/solution.py
+++ b/solution.py
@@ -5,6 +5,11 @@
 from jax.sharding import PartitionSpec as P
 
 PRECISE = lax.Precision.HIGHEST
+
+
+def gather_over(shard, mesh_axis, dim):
+    stack = jnp.stack([shard] * lax.axis_size(mesh_axis))
+    return jnp.concatenate(lax.all_to_all(stack, mesh_axis, 0, 0), axis=dim)
 
 
 def passed_along(block, axis, distance):
@@ -152,7 +157,7 @@
     mixed = convolution + skip[:, None] * gated
     out_gate = convolved[0] * mixed
     columns = w_out
-    output = jnp.dot(columns, lax.all_gather(out_gate, "ch", axis=0, tiled=True), precision=PRECISE)
+    output = jnp.dot(columns, gather_over(out_gate, "ch", 0), precision=PRECISE)
     columns = w_out
     grad_gate = lax.psum_scatter(
         jnp.dot(columns.T, cotangent, precision=PRECISE), "ch", scatter_dimension=0, tiled=True

time: 440 us -> 439 us (level)
    all_to_all x0 -> x1, blocking collectives: none -> 21 us  [gather_over(): return jnp.concatenate(lax.all_to_all(stack, mesh_axis, 0, 0), axis=dim)]
    all_gather x1 -> x0, blocking collectives: 17.1 us -> none  [body(): lax.all_gather(out_gate, 'ch', axis=0, tiled=True)]
    unnamed x46 -> x52, local copies, waits for them, and re-layouts: 14.1 us -> 13.3 us
where the time goes in v1:
time: 439 us; the launch traced here: 432 us
  blocking collectives  203 us (46%)
  matrix products  92.7 us (21%)
  waiting for transfers between devices  50.5 us (12%)
  starting transfers between devices  33.2 us (8%)
  other arithmetic  19.5 us (4%)
  local copies, waits for them, and re-layouts  18.2 us (4%)
  between operations  15.2 us (3%)
    all_to_all x2, blocking collectives, to_spectrum(): lax.all_to_all(stacked, 'seq', split_axis=2, concat_axis=2, tiled=True)  41.5 us
    all_to_all x2, blocking collectives, to_sorted(): lax.all_to_all(stacked, 'seq', split_axis=2, concat_axis=2, tiled=True)  38.4 us
    all_to_all x2, blocking collectives, from_spectrum(): lax.all_to_all(pieces, 'seq', split_axis=2, concat_axis=2, tiled=True)  33.3 us
    all_to_all x1, blocking collectives, gather_over(): return jnp.concatenate(lax.all_to_all(stack, mesh_axis, 0, 0), axis=dim)  21 us
    all_to_all x1, blocking collectives, from_spectrum(): lax.all_to_all(stacked, 'seq', split_axis=2, concat_axis=2, tiled=True)  19.9 us
    all_to_all x1, blocking collectives, to_spectrum(): lax.all_to_all(signal.reshape(rows_in, channels, shards, slab_len), 'seq'...  19.7 us
    all_to_all x1, blocking collectives, from_sorted(): lax.all_to_all(stacked, 'seq', split_axis=2, concat_axis=2, tiled=True)  19.1 us
    all_to_all x1, starting transfers between devices, to_spectrum(): lax.all_to_all(signal.reshape(rows_in, channels, shards, slab_len), 'seq'...  17.3 us
  transfers between devices with their start and end apart: 7, of which 6 were waited for; matrix products, arithmetic and copies ran while one was open for 2% of the time, Pallas kernels for 0%

profile of v1, /device:TPU:1, one launch (start us, length us, event | category | flops | bytes accessed | tf_op | source)
XLA Modules:
  0.0 432.1 jit_solution(10710695608534171154)
XLA Ops:
  7.2 9.9 %all_gather.3 = f32[256,512]{1,0:T(8,128)S(1)} all-gather(f32[64,512]{1,0:T(8,128)} %param.7), channel_id=1, replica_groups=mesh['seq'=64,'ch'=4] {'ch'}, dimensions={0}, use_global_device_ids=true | all-gather | bytes 655360 | tf_op jit(solution)/shard_map/all_gather | solution.py:137
  23.8 17.3 %all-to-all-start = ((f32[64,1,1024]{2,1,0:T(1,128)}), f32[64,1,1024]{2,1,0:T(1,128)S(1)}, u32[]{:S(2)}, u32[]{:S(2)}) async-start(f32[64,1,1024]{2,1,0:T(1,128)} %reshape.229), calls=%async_computation | async-start | bytes 524288 | tf_op jit(solution)/shard_map/all_to_all | solution.py:58
  41.3 13.2 %all-to-all-done = f32[64,1,1024]{2,1,0:T(1,128)S(1)} async-done(((f32[64,1,1024]{2,1,0:T(1,128)}), f32[64,1,1024]{2,1,0:T(1,128)S(1)}, u32[]{:S(2)}, u32[]{:S(2)}) %all-to-all-start) | async-done | bytes 262176 | tf_op jit(solution)/shard_map/all_to_all | solution.py:58
  59.8 24.5 %all_to_all.65 = f32[64,1,2048]{2,1,0:T(1,128)S(1)} all-to-all(f32[64,1,2048]{2,1,0:T(1,128)S(1)} %reshape.231), channel_id=1, replica_groups=mesh['seq'=64,'ch'=4] {'seq'}, dimensions={0} | all-to-all | bytes 1048576 | tf_op jit(solution)/shard_map/all_to_all | solution.py:78
  86.7 5.4 %fusion.19 = f32[2,64,512]{2,1,0:T(8,128)S(1)} fusion(f32[2,64,64,8]{1,3,0,2:T(8,128)S(1)} %get-tuple-element.24), kind=kOutput, calls=%fused_computation.40 | convolution fusion | flops 406323200 | bytes 524288 | tf_op jit(solution)/shard_map/ncj,jk->nck/dot_general | solution.py:83
  92.1 5.4 %fusion.17 = f32[2,64,512]{2,1,0:T(8,128)S(1)} fusion(f32[2,64,64,8]{1,3,0,2:T(8,128)S(1)} %get-tuple-element.25), kind=kOutput, calls=%fused_computation.38 | convolution fusion | flops 406323200 | bytes 524288 | tf_op jit(solution)/shard_map/ncj,jk->nck/dot_general | solution.py:86
  97.6 5.5 %convolution_add_fusion.1 = f32[2,64,512]{2,1,0:T(8,128)S(1)} fusion(f32[2,64,512]{2,1,0:T(8,128)S(1)} %fusion.19, f32[2,64,64,8]{1,3,0,2:T(8,128)S(1)} %get-tuple-element.25), kind=kOutput, calls=%fused_computation.16 | convolution fusion | flops 406388736 | bytes 786432 | tf_op jit(solution)/shard_map/ncj,jk->nck/dot_general | solution.py:83
  103.0 5.7 %convolution_subtract_fusion.3 = f32[2,64,512]{2,1,0:T(8,128)S(1)} fusion(f32[2,64,512]{2,1,0:T(8,128)S(1)} %fusion.17, f32[2,64,64,8]{1,3,0,2:T(8,128)S(1)} %get-tuple-element.24), kind=kOutput, calls=%fused_computation.15 | convolution fusion | flops 406388736 | bytes 786432 | tf_op jit(solution)/shard_map/ncj,jk->nck/dot_general | solution.py:86
  109.9 21.4 %all_to_all.66 = f32[64,1,2048]{2,1,0:T(1,128)S(1)} all-to-all(f32[64,1,2048]{2,1,0:T(1,128)S(1)} %reshape.233), channel_id=1, replica_groups=mesh['seq'=64,'ch'=4] {'seq'}, dimensions={0} | all-to-all | bytes 1048576 | tf_op jit(solution)/shard_map/all_to_all | solution.py:34
  134.9 7.1 %all-to-all-start.3 = ((f32[64,1,1024]{2,1,0:T(1,128)}), f32[64,1,1024]{2,1,0:T(1,128)S(1)}, u32[]{:S(2)}, u32[]{:S(2)}) async-start(f32[64,1,1024]{2,1,0:T(1,128)} %reshape.235), calls=%async_computation.3 | async-start | bytes 524288 | tf_op jit(solution)/shard_map/all_to_all | solution.py:46
  142.0 12.3 %all-to-all-done.3 = f32[64,1,1024]{2,1,0:T(1,128)S(1)} async-done(((f32[64,1,1024]{2,1,0:T(1,128)}), f32[64,1,1024]{2,1,0:T(1,128)S(1)}, u32[]{:S(2)}, u32[]{:S(2)}) %all-to-all-start.3) | async-done | bytes 262176 | tf_op jit(solution)/shard_map/all_to_all | solution.py:46
  182.9 10.5 %all-to-all-done.4 = f32[64,1,1024]{2,1,0:T(1,128)S(1)} async-done(((f32[64,1,1024]{2,1,0:T(1,128)}), f32[64,1,1024]{2,1,0:T(1,128)S(1)}, u32[]{:S(2)}, u32[]{:S(2)}) %all-to-all-start.4) | async-done | bytes 262176 | tf_op jit(solution)/shard_map/all_to_all | solution.py:117
  196.5 15.9 %all_to_all.67 = f32[64,1,512]{2,1,0:T(1,128)S(1)} all-to-all(f32[64,1,512]{2,1,0:T(1,128)S(1)} %reshape.239), channel_id=1, replica_groups=mesh['seq'=64,'ch'=4] {'seq'}, dimensions={0} | all-to-all | bytes 262144 | tf_op jit(solution)/shard_map/all_to_all | solution.py:124
  215.5 19.7 %all_to_all.68 = f32[64,1,512]{2,1,0:T(1,128)S(1)} all-to-all(f32[64,1,512]{2,1,0:T(1,128)S(1)} %reshape.241), channel_id=1, replica_groups=mesh['seq'=64,'ch'=4] {'seq'}, dimensions={0} | all-to-all | bytes 262144 | tf_op jit(solution)/shard_map/all_to_all | solution.py:58
  238.1 17.0 %all_to_all.69 = f32[64,1,1024]{2,1,0:T(1,128)S(1)} all-to-all(f32[64,1,1024]{2,1,0:T(1,128)S(1)} %reshape.243), channel_id=1, replica_groups=mesh['seq'=64,'ch'=4] {'seq'}, dimensions={0} | all-to-all | bytes 524288 | tf_op jit(solution)/shard_map/all_to_all | solution.py:78
  276.5 16.9 %all_to_all.70 = f32[64,1,1024]{2,1,0:T(1,128)S(1)} all-to-all(f32[64,1,1024]{2,1,0:T(1,128)S(1)} %reshape.245), channel_id=1, replica_groups=mesh['seq'=64,'ch'=4] {'seq'}, dimensions={0} | all-to-all | bytes 524288 | tf_op jit(solution)/shard_map/all_to_all | solution.py:34
  295.7 19.1 %all_to_all.71 = f32[64,1,2048]{2,1,0:T(1,128)S(1)} all-to-all(f32[64,1,2048]{2,1,0:T(1,128)S(1)} %reshape.247), channel_id=1, replica_groups=mesh['seq'=64,'ch'=4] {'seq'}, dimensions={0} | all-to-all | bytes 1048576 | tf_op jit(solution)/shard_map/all_to_all | solution.py:46
  322.7 5.4 %fusion.15 = f32[2,64,512]{2,1,0:T(8,128)S(1)} fusion(f32[2,64,64,8]{1,3,0,2:T(8,128)S(1)} %get-tuple-element.21), kind=kOutput, calls=%fused_computation.36 | convolution fusion | flops 406323200 | bytes 524288 | tf_op jit(solution)/shard_map/nck,kj->ncj/dot_general | solution.py:100
  328.1 5.5 %convolution_subtract_fusion.1 = f32[2,64,512]{2,1,0:T(8,128)S(1)} fusion(f32[2,64,512]{2,1,0:T(8,128)S(1)} %fusion.15, f32[2,64,64,8]{1,3,0,2:T(8,128)S(1)} %get-tuple-element.20), kind=kOutput, calls=%fused_computation.11 | convolution fusion | flops 406388736 | bytes 786432 | tf_op jit(solution)/shard_map/nck,kj->ncj/dot_general | solution.py:100
  333.6 5.7 %multiply_subtract_fusion.1 = (f32[2,64,512]{2,1,0:T(8,128)S(1)}, f32[2,64,512]{2,1,0:T(8,128)S(1)}) fusion(f32[2,64,512]{2,1,0:T(8,128)S(1)} %convolution_subtract_fusion.1, f32[512]{0:T(512)S(1)} %copy-done.7, f32[512]{0:T(512)S(1)} %copy-done.9, f32[2,64,512]{2,1,0:T(8,128)S(1)} %fusion.13, f32[2,64,64,8]{1,3,0,2:T(8,128)S(1)} %get-tuple-element.21), kind=kOutput, calls=%fused_computation.109 | convolution fusion | flops 406781952 | bytes 1314816 | tf_op jit(solution)/shard_map/nck,kj->ncj/dot_general | solution.py:103
  340.5 19.9 %all_to_all.72 = f32[64,1,2048]{2,1,0:T(1,128)S(1)} all-to-all(f32[64,1,2048]{2,1,0:T(1,128)S(1)} %reshape.249), channel_id=1, replica_groups=mesh['seq'=64,'ch'=4] {'seq'}, dimensions={0} | all-to-all | bytes 1048576 | tf_op jit(solution)/shard_map/all_to_all | solution.py:117
  365.7 17.4 %all_to_all.73 = f32[64,1,1024]{2,1,0:T(1,128)S(1)} all-to-all(f32[64,1,1024]{2,1,0:T(1,128)S(1)} %reshape.251), channel_id=1, replica_groups=mesh['seq'=64,'ch'=4] {'seq'}, dimensions={0} | all-to-all | bytes 524288 | tf_op jit(solution)/shard_map/all_to_all | solution.py:124
  393.1 21.0 %all_to_all.74 = f32[4,64,512]{2,1,0:T(8,128)S(1)} all-to-all(f32[4,64,512]{2,1,0:T(8,128)S(1)} %stack.38), channel_id=1, replica_groups=mesh['seq'=64,'ch'=4] {'ch'}, dimensions={0} | all-to-all | bytes 1048576 | tf_op jit(solution)/shard_map/all_to_all | solution.py:12
  416.0 9.1 %reduce-scatter.7.cloned.1.call-done = f32[64,512]{1,0:T(8,128)} async-done(((f32[256,512]{1,0:T(8,128)}), f32[64,512]{1,0:T(8,128)}) %reduce-scatter.7.cloned.1.call-update) | async-done | bytes 131088
  (148 shorter events, 106.0 us)
Async XLA Ops:
  7.2 9.9 %copy-start = (f32[3,64,256]{2,1,0:T(8,128)S(1)}, f32[3,64,256]{2,1,0:T(8,128)}, u32[]{:S(2)}) copy-start(f32[3,64,256]{2,1,0:T(8,128)} %param.8) | copy-start | bytes 589828
  17.6 2.6 copy-start.2
  17.7 4.5 %collective-permute-start = (f32[3,64,2]{2,1,0:T(8,128)S(1)}, f32[3,64,2]{2,1,0:T(8,128)S(1)}, u32[]{:S(2)}, u32[]{:S(2)}) collective-permute-start(f32[3,64,2]{2,1,0:T(8,128)S(1)} %slice.167), channel_id=1, source_target_pairs={{0,4},{4,8},{8,12},{12,16},{16,20},{20,24},{24,28},{28,32},{32,36}... | collective-permute-start | bytes 4616 | tf_op jit(solution)/shard_map/ppermute | solution.py:18
  20.3 0.7 copy-start.4
  23.8 30.6 %all-to-all-start = ((f32[64,1,1024]{2,1,0:T(1,128)}), f32[64,1,1024]{2,1,0:T(1,128)S(1)}, u32[]{:S(2)}, u32[]{:S(2)}) async-start(f32[64,1,1024]{2,1,0:T(1,128)} %reshape.229), calls=%async_computation | async-start | bytes 524288 | tf_op jit(solution)/shard_map/all_to_all | solution.py:58
  134.9 19.4 %all-to-all-start.3 = ((f32[64,1,1024]{2,1,0:T(1,128)}), f32[64,1,1024]{2,1,0:T(1,128)S(1)}, u32[]{:S(2)}, u32[]{:S(2)}) async-start(f32[64,1,1024]{2,1,0:T(1,128)} %reshape.235), calls=%async_computation.3 | async-start | bytes 524288 | tf_op jit(solution)/shard_map/all_to_all | solution.py:46
  142.0 28.2 %copy-start.6 = (f32[512]{0:T(512)}, f32[512]{0:T(512)S(1)}, u32[]{:S(2)}) copy-start(f32[512]{0:T(512)S(1)} %get-tuple-element.45) | copy-start | bytes 6148
  142.0 28.2 %copy-start.8 = (f32[512]{0:T(512)}, f32[512]{0:T(512)S(1)}, u32[]{:S(2)}) copy-start(f32[512]{0:T(512)S(1)} %get-tuple-element.46) | copy-start | bytes 6148
  176.4 5.0 %copy-start.1 = (f32[64,256]{1,0:T(8,128)S(1)}, f32[64,256]{1,0:T(8,128)}, u32[]{:S(2)}) copy-start(f32[64,256]{1,0:T(8,128)} %param.12) | copy-start | bytes 196612
  176.4 5.0 %copy-start.3 = (f32[64,512]{1,0:T(8,128)S(1)}, f32[64,512]{1,0:T(8,128)}, u32[]{:S(2)}) copy-start(f32[64,512]{1,0:T(8,128)} %param.13) | copy-start | bytes 393220
  176.4 17.0 %all-to-all-start.4 = ((f32[64,1,1024]{2,1,0:T(1,128)}), f32[64,1,1024]{2,1,0:T(1,128)S(1)}, u32[]{:S(2)}, u32[]{:S(2)}) async-start(f32[64,1,1024]{2,1,0:T(1,128)} %reshape.237), calls=%async_computation.4 | async-start | bytes 524288 | tf_op jit(solution)/shard_map/all_to_all | solution.py:117
  181.2 32.5 %reduce-scatter.5.cloned.1.call-start = ((), (), s32[]{:S(2)}) async-start(), calls=%async_computation.15 | async-start | bytes 655360 | tf_op jit(solution)/shard_map/reduce_scatter | solution.py:162
  182.8 242.2 %reduce-scatter.7.cloned.1.call-start = ((), (), s32[]{:S(2)}) async-start(), calls=%async_computation.16 | async-start | bytes 655360
  213.5 0.7 copy-start.5
  328.1 5.5 %copy-start.7 = (f32[512]{0:T(512)S(1)}, f32[512]{0:T(512)}, u32[]{:S(2)}) copy-start(f32[512]{0:T(512)} %copy-done.6) | copy-start | bytes 6148
  328.1 5.5 %copy-start.9 = (f32[512]{0:T(512)S(1)}, f32[512]{0:T(512)}, u32[]{:S(2)}) copy-start(f32[512]{0:T(512)} %copy-done.8) | copy-start | bytes 6148
  384.9 5.7 %collective-permute-start.1 = (f32[3,64,2]{2,1,0:T(8,128)S(1)}, f32[3,64,2]{2,1,0:T(8,128)S(1)}, u32[]{:S(2)}, u32[]{:S(2)}) collective-permute-start(f32[3,64,2]{2,1,0:T(8,128)S(1)} %slice.192), channel_id=1, source_target_pairs={{4,0},{8,4},{12,8},{16,12},{20,16},{24,20},{28,24},{32,28},{36,32}... | collective-permute-start | bytes 4616 | tf_op jit(solution)/shard_map/ppermute | solution.py:18
Sparse Core Ops, SparseCore 0:
  184.5 26.0 reduce-scatter.4
  393.0 32.0 reduce-scatter.6
